TPU v7x, 32 devices: a whole 2x2x4 slice. The times are simulated.
32 devices in a mesh: parts: 2 (over x), ctx: 8 (over z, y), head: 2 (over core).
Axes of the slice: x: 2, y: 2, z: 4, core: 2. Of those that a mesh axis runs over, the one named last changes fastest.
Arguments:
- channels: bfloat16 [2048, 2048], P(('parts', 'ctx'), 'head'), parts along dimension 0, may hold values from -6 to 6
- gate_channels: bfloat16 [2048, 2048], P(('parts', 'ctx'), 'head'), parts along dimension 0, may hold values from -6 to 6
- bmat: bfloat16 [2048, 512], P(('parts', 'ctx'), 'head'), parts along dimension 0, may hold values from -4 to 4
- cmat: bfloat16 [2048, 512], P(('parts', 'ctx'), 'head'), parts along dimension 0, may hold values from -4 to 4
- dt: float32 [2048, 32], P(('parts', 'ctx'), 'head'), parts along dimension 0, may hold values from 0.1 to 40
- rates: float32 [32], P('head'), may hold values from 0.00029296876 to 0.03
- skip: float32 [32], P('head'), may hold values from 0.5 to 2
- norm_gain: float32 [2048], P('head'), may hold values from 0.25 to 1.75
- docs: int32 [2048], P(('parts', 'ctx')), parts along dimension 0, may hold values from 0 to 3, never falling along the last dimension, each value on 1 to 512 neighbouring positions
- w_out: bfloat16 [2048, 2688], P('head', 'ctx'), may hold values from -0.125 to 0.125
- residual: bfloat16 [2048, 2688], P(('parts', 'ctx', 'head')), parts along dimension 0, may hold values from -6 to 6
- moe_gain: float32 [2688], replicated, may hold values from 0.25 to 1.75
- experts: int32 [2048, 6], P(('parts', 'ctx', 'head')), parts along dimension 0, may hold values from 0 to 15, all different within a row; in each aligned block of 64 rows (0 to 63, 64 to 127, ...) at most 36 rows name the same one
- gates: float32 [2048, 6], P(('parts', 'ctx', 'head')), parts along dimension 0, may hold values from 0.05 to 0.5
- w_up: bfloat16 [16, 2688, 928], P(('ctx', 'head')), may hold values from -0.125 to 0.125
- w_down: bfloat16 [16, 928, 2688], P(('ctx', 'head')), may hold values from -0.1875 to 0.1875
Outputs:
- layer_out: bfloat16 [2048, 2688], P(('parts', 'ctx', 'head')), parts along dimension 0
There are 2 independent parts, one for each index of `parts`. A program takes and returns all parts, laid end to end along the dimension named above; an argument that names none is the same for every part. Nothing has to cross between parts.
Inputs may be any that keep to these rules, and one draw needn't show every extreme that they name: Each row names 6 different experts; in each aligned block of 64 rows (the rows of one device) no expert is named by more than 36 rows. `docs`: ids never fall along the tokens; a document starts where the id changes and holds at most half of the 1024 tokens.
All inputs are finite; a program needn't handle non-finite values.
Results may differ from a plain program's by a relative error of at most 0.013.
Values may be sent and summed in bfloat16 or wider, within the bound.
No kernel may reach another device: no remote copies, remote signals or barrier semaphores. Data moves between devices by JAX's collectives and lax.ppermute only.
A program may use at most 128 MiB of HBM per device.

v0:
```python
import jax
import jax.numpy as jnp
from jax import lax
from jax.sharding import PartitionSpec as P

HEADS = 32
HEAD_DIM = 64
GROUPS = 4
STATE = 128
EPS = 1e-05


def entering(array, axis, combine, identity):
    size, place = (lax.axis_size(axis), lax.axis_index(axis))
    everything = jax.tree.map(lambda part: lax.all_gather(part, axis), array)
    start = jax.tree.map(
        lambda part, zero: jnp.broadcast_to(jnp.asarray(zero, part.dtype), part.shape),
        array,
        identity,
    )

    def lap(k, before):
        reached = k < place
        new = combine(before, jax.tree.map(lambda part: part[k], everything))
        return jax.tree.map(lambda a, b: jnp.where(reached, a, b), new, before)

    return lax.fori_loop(0, size, lap, start)


def silu(value):
    return value / (1.0 + jnp.exp(-value))


def combine_states(earlier, later):
    first_a, last_a, decay_a, state_a = earlier
    first_b, last_b, decay_b, state_b = later
    linked = ((last_a == first_b) | (last_a < 0) | (first_b < 0)).astype(jnp.float32)
    carried = decay_b * linked
    decay = carried * decay_a
    state = state_b + carried[:, None, None] * state_a
    first = jnp.where(first_a < 0, first_b, first_a)
    last = jnp.where(last_b < 0, last_a, last_b)
    return (first, last, decay, state)


def group_terms(inputs, causal, ending):
    x_group, b_group, c_group, log_group, dt_group = inputs
    scores = jnp.dot(c_group, b_group.T, preferred_element_type=jnp.float32)
    gap = jnp.where(causal[:, :, None], log_group[:, None, :] - log_group[None, :, :], -jnp.inf)
    weight = jnp.exp(gap) * scores[:, :, None] * dt_group[None, :, :]
    inner = jnp.einsum("tsh,shp->thp", weight, x_group, precision=lax.Precision.HIGHEST)
    tail = jnp.exp(log_group[-1][None, :] - log_group) * ending[:, None] * dt_group
    end_state = jnp.einsum(
        "sh,shp,sn->hpn",
        tail,
        x_group,
        b_group.astype(jnp.float32),
        precision=lax.Precision.HIGHEST,
    )
    return (inner, end_state)


def expert_rows(received, up_weight, down_weight):
    sources, items, width = received.shape
    rows = received.reshape(sources * items, width)
    up = jnp.dot(rows, up_weight, preferred_element_type=jnp.float32)
    act = jnp.square(jnp.maximum(up, 0.0)).astype(jnp.bfloat16)
    result = jnp.dot(act, down_weight, preferred_element_type=jnp.float32).astype(jnp.bfloat16)
    return result.reshape(sources, items, width)


def local(
    channels,
    gate_channels,
    bmat,
    cmat,
    dt,
    rates,
    skip,
    norm_gain,
    docs,
    w_out,
    residual,
    moe_gain,
    experts,
    gates,
    w_up,
    w_down,
):
    length = channels.shape[0]
    heads = dt.shape[1]
    groups = bmat.shape[1] // STATE
    per_group = heads // groups
    logs = jnp.cumsum(-rates[None, :] * dt, axis=0)
    x_wide = channels.astype(jnp.float32).reshape(length, groups, per_group, HEAD_DIM)
    b_split = bmat.reshape(length, groups, STATE)
    c_split = cmat.reshape(length, groups, STATE)
    position = jnp.arange(length, dtype=jnp.int32)
    causal = (docs[:, None] == docs[None, :]) & (position[:, None] >= position[None, :])
    ending = (docs == docs[length - 1]).astype(jnp.float32)
    opening = (docs == docs[0]).astype(jnp.float32)
    stacked = (
        x_wide.transpose(1, 0, 2, 3),
        b_split.transpose(1, 0, 2),
        c_split.transpose(1, 0, 2),
        logs.reshape(length, groups, per_group).transpose(1, 0, 2),
        dt.reshape(length, groups, per_group).transpose(1, 0, 2),
    )
    inner, end_state = lax.map(lambda item: group_terms(item, causal, ending), stacked)
    end_state = end_state.reshape(heads, HEAD_DIM, STATE)
    whole_decay = jnp.exp(logs[length - 1]) * (docs[0] == docs[length - 1]).astype(jnp.float32)
    element = (docs[:1], docs[length - 1 :], whole_decay, end_state)
    identity = (
        jnp.full((1,), -1, jnp.int32),
        jnp.full((1,), -1, jnp.int32),
        jnp.ones((heads,), jnp.float32),
        jnp.zeros_like(end_state),
    )
    _, prior_last, _, incoming = entering(element, "ctx", combine_states, identity)
    linked = (prior_last == docs[:1]).astype(jnp.float32)
    reach = jnp.exp(logs) * opening[:, None] * linked
    outer = jnp.einsum(
        "tgn,ghpn->tghp",
        c_split.astype(jnp.float32),
        incoming.reshape(groups, per_group, HEAD_DIM, STATE),
        precision=lax.Precision.HIGHEST,
    )
    outer = outer * reach.reshape(length, groups, per_group)[:, :, :, None]
    inner = inner.transpose(1, 0, 2, 3)
    scan = (inner + outer).reshape(length, heads, HEAD_DIM) + skip[None, :, None] * x_wide.reshape(
        length, heads, HEAD_DIM
    )
    scan = scan.reshape(length, heads * HEAD_DIM)
    gated = scan * silu(gate_channels.astype(jnp.float32))
    grouped = gated.reshape(length, -1, HEADS * HEAD_DIM // GROUPS)
    grouped = grouped / jnp.sqrt(jnp.mean(grouped * grouped, axis=2, keepdims=True) + EPS)
    normed_scan = (grouped.reshape(length, -1) * norm_gain).astype(jnp.bfloat16)
    partial_value = jnp.dot(
        normed_scan,
        lax.all_gather(w_out, "ctx", axis=1, tiled=True),
        preferred_element_type=jnp.float32,
    )
    mamba_out = lax.psum_scatter(
        partial_value.astype(jnp.bfloat16), "head", scatter_dimension=0, tiled=True
    ).astype(jnp.float32)
    hidden = (residual.astype(jnp.float32) + mamba_out).astype(jnp.bfloat16)
    widened = hidden.astype(jnp.float32)
    moe_in = (
        widened / jnp.sqrt(jnp.mean(widened * widened, axis=1, keepdims=True) + EPS) * moe_gain
    ).astype(jnp.bfloat16)
    rows_dev = moe_in.shape[0]
    top = experts.shape[1]
    width = moe_in.shape[1]
    ctx_count = lax.axis_size("ctx")
    head_count = lax.axis_size("head")
    experts_all = ctx_count * head_count
    capacity = min(rows_dev, max(4, 3 * rows_dev * top // (2 * experts_all)))
    picks = experts.reshape(-1)
    pick_index = jnp.arange(picks.shape[0], dtype=jnp.int32)
    earlier = (picks[:, None] == picks[None, :]) & (pick_index[None, :] < pick_index[:, None])
    slot = jnp.sum(earlier.astype(jnp.int32), axis=1)
    target = (picks * capacity + slot).reshape(rows_dev, top)
    places = jnp.arange(experts_all * capacity, dtype=jnp.int32)
    routing = jnp.any(target[None, :, :] == places[:, None, None], axis=2).astype(jnp.bfloat16)
    outgoing = jnp.dot(routing, moe_in, preferred_element_type=jnp.float32).astype(jnp.bfloat16)
    outgoing = outgoing.reshape(experts_all, capacity, width)
    up_weight = w_up[0]
    down_weight = w_down[0]
    results = expert_rows(
        lax.all_to_all(outgoing, ("ctx", "head"), split_axis=0, concat_axis=0, tiled=True),
        up_weight,
        down_weight,
    )
    returned = lax.all_to_all(results, ("ctx", "head"), split_axis=0, concat_axis=0, tiled=True)
    flat_back = returned.reshape(experts_all * capacity, width)
    chosen = flat_back[target].astype(jnp.float32)
    mixture = jnp.sum(chosen * gates[:, :, None], axis=1)
    return (widened + mixture).astype(jnp.bfloat16)


def solution(mesh):
    return jax.shard_map(
        local,
        mesh=mesh,
        in_specs=(
            P(("parts", "ctx"), "head"),
            P(("parts", "ctx"), "head"),
            P(("parts", "ctx"), "head"),
            P(("parts", "ctx"), "head"),
            P(("parts", "ctx"), "head"),
            P("head"),
            P("head"),
            P("head"),
            P(("parts", "ctx")),
            P("head", "ctx"),
            P(("parts", "ctx", "head"), None),
            P(),
            P(("parts", "ctx", "head"), None),
            P(("parts", "ctx", "head"), None),
            P(("ctx", "head"), None, None),
            P(("ctx", "head"), None, None),
        ),
        out_specs=P(("parts", "ctx", "head"), None),
        check_vma=False,
    )
```

profile of v0, /device:TPU:13, one launch (start us, length us, event | category | flops | bytes accessed | tf_op | source)
XLA Modules:
  0.0 410.6 jit_solution(10175892320558822707)
XLA Ops:
  12.6 1.9 fusion.64
  14.5 1.8 compare_convert_fusion
  16.2 6.9 %while.29 = (s32[]{:T(128)}, f32[2,128,8,64]{1,3,2,0:T(8,128)S(1)}, f32[2,8,64,128]{3,2,1,0:T(8,128)S(1)}, f32[2,128,8,64]{1,3,2,0:T(8,128)S(1)}, f32[2,128,8]{1...) while((s32[]{:T(128)}, f32[2,128,8,64]{1,3,2,0:T(8,128)S(1)}, ...), condition=%wide.region_2.3_spmd.clone, body=%wide.region_1.2_spmd.clone.sunk | while | flops 206162944 | bytes 1364697 | solution.py:109
  24.8 1.4 slice_dynamic-update-slice_fusion
  26.2 7.9 %all-reduce.2 = (s32[8]{0:T(128)S(1)}, s32[8]{0:T(128)S(1)}) all-reduce(s32[8]{0:T(128)S(1)} %get-tuple-element.359, s32[8]{0:T(128)S(1)} %slice_dynamic-update-slice_fusion), channel_id=2, replica_groups=mesh['parts'=2,'ctx'=8,'head'=2] {'ctx'}, use_global_device_ids=true, to_apply=%add | all-reduce | flops 16 | bytes 128
  35.3 12.1 %all-gather.2 = f32[8,1,16]{2,1,0:T(1,128)S(1)} all-gather(f32[1,1,16]{2,1,0:T(1,128)S(1)} %fusion.61), channel_id=1, replica_groups=mesh['parts'=2,'ctx'=8,'head'=2] {'ctx'}, dimensions={0}, use_global_device_ids=true | all-gather | bytes 576 | tf_op jit(solution)/shard_map/all_gather | solution.py:15
  47.4 47.7 %all-gather.6.cloned.1.call-done = f32[8,16,64,128]{3,2,1,0:T(8,128)} async-done(((f32[1,16,64,128]{3,2,1,0:T(8,128)}), f32[8,16,64,128]{3,2,1,0:T(8,128)}) %all-gather.6.cloned.1.call-update) | async-done | bytes 4194320 | tf_op jit(solution)/shard_map/all_gather | solution.py:15
  95.1 35.5 %while.30 = (s32[]{:T(128)}, s32[1]{0:T(128)}, f32[16,64,128]{2,1,0:T(8,128)S(1)}, s32[]{:T(128)}, s32[8,1]{0,1:T(1,128)S(1)}, /*index=5*/f32[8,16,64,128]{3,2,1...) while((s32[]{:T(128)}, s32[1]{0:T(128)}, ...), condition=%wide.region_4.5_spmd.clone, body=%wide.region_3.4_spmd.clone.sunk | while | flops 524317 | bytes 1573290 | solution.py:27
  133.0 51.6 %all-gather.8.cloned.1.call-done = bf16[1024,2688]{0,1:T(8,128)(2,1)} async-done(((bf16[1024,336]{0,1:T(8,128)(2,1)}), bf16[1024,2688]{0,1:T(8,128)(2,1)}) %all-gather.8.cloned.1.call-update) | async-done | bytes 5505040 | tf_op jit(solution)/shard_map/all_gather | solution.py:140
  184.7 5.4 %convolution_convert_fusion.1 = bf16[128,2688]{1,0:T(8,128)(2,1)} fusion(bf16[1024,2688]{0,1:T(8,128)(2,1)} %all-gather.8.cloned.1.call-done, f32[128,1024]{1,0:T(8,128)S(1)} %bitcast.145, f32[1024]{0:T(1024)S(1)} %copy-done.10, bf16[128,1024]{1,0:T(8,128)(2,1)S(1)} %copy-done.5, f32[128,1024]{1,0:T(8,128)S(1)} %copy.99, f32[1024]{0:T(1024)S(1)} %mul.206, ...), kind=kOutput, calls=%fused_computation.53 | convolution fusion | flops 706428928 | bytes 7774208 | tf_op jit(solution)/shard_map/dot_general | solution.py:138
  191.0 9.5 %reduce-scatter.2.cloned.1.call-done = bf16[64,2688]{1,0:T(8,128)(2,1)} async-done(((bf16[128,2688]{1,0:T(8,128)(2,1)}), bf16[64,2688]{1,0:T(8,128)(2,1)}) %reduce-scatter.2.cloned.1.call-update) | async-done | bytes 344080 | tf_op jit(solution)/shard_map/reduce_scatter | solution.py:143
  201.7 2.0 convolution_convert_fusion
  203.8 2.5 reshape.115
  206.2 81.9 %all_to_all.10 = bf16[16,36,2688]{2,1,0:T(8,128)(2,1)S(1)} all-to-all(bf16[16,36,2688]{2,1,0:T(8,128)(2,1)} %reshape.115), channel_id=1, replica_groups=mesh['parts'=2,'ctx'=8,'head'=2] {'ctx','head'}, dimensions={0} | all-to-all | bytes 6193152 | tf_op jit(solution)/shard_map/all_to_all | solution.py:170
  288.1 2.4 reshape.116
  290.5 6.9 %multiply_convert_fusion = bf16[576,928]{1,0:T(8,128)(2,1)S(1)} fusion(bf16[576,2688]{1,0:T(8,128)(2,1)} %reshape.116, bf16[1,2688,928]{1,2,0:T(8,128)(2,1)} %param.34), kind=kOutput, calls=%fused_computation.54 | convolution fusion | flops 2875226112 | bytes 9154560 | tf_op jit(solution)/shard_map/dot_general | solution.py:66
  297.4 6.2 %fusion.38 = bf16[576,2688]{1,0:T(8,128)(2,1)S(1)} fusion(bf16[576,928]{1,0:T(8,128)(2,1)S(1)} %multiply_convert_fusion, bf16[1,928,2688]{2,1,0:T(8,128)(2,1)} %param.35), kind=kOutput, calls=%fused_computation.51 | convolution fusion | flops 2875170816 | bytes 9154560 | tf_op jit(solution)/shard_map/dot_general | solution.py:68
  303.5 2.5 reshape.117
  306.1 5.3 %all-to-all-start.1 = ((bf16[16,36,2688]{2,1,0:T(8,128)(2,1)}), bf16[16,36,2688]{2,1,0:T(8,128)(2,1)}, u32[]{:S(2)}, u32[]{:S(2)}) async-start(bf16[16,36,2688]{2,1,0:T(8,128)(2,1)} %reshape.117), calls=%async_computation.2 | async-start | bytes 6881280 | tf_op jit(solution)/shard_map/all_to_all | solution.py:174
  311.7 76.0 %all-to-all-done.1 = bf16[16,36,2688]{2,1,0:T(8,128)(2,1)} async-done(((bf16[16,36,2688]{2,1,0:T(8,128)(2,1)}), bf16[16,36,2688]{2,1,0:T(8,128)(2,1)}, u32[]{:S(2)}, u32[]{:S(2)}) %all-to-all-start.1) | async-done | bytes 3096608 | tf_op jit(solution)/shard_map/all_to_all | solution.py:174
  387.7 3.0 reshape.118
  390.6 3.4 gather_fusion
  394.1 4.5 %reshape.133 = f32[64,6,2688]{2,1,0:T(8,128)} reshape(bf16[384,2688]{1,0:T(8,128)(2,1)} %gather_fusion) | data formatting | bytes 6193152 | tf_op jit(solution)/shard_map/convert_element_type | solution.py:176
  398.6 4.6 %multiply_reduce_fusion = f32[64,2688]{1,0:T(8,128)S(1)} fusion(f32[64,6,2688]{2,1,0:T(8,128)} %reshape.133, f32[64,6]{1,0:T(8,128)S(1)} %copy.105), kind=kLoop, calls=%fused_computation.46 | loop fusion | flops 1892352 | bytes 4818432 | tf_op jit(solution)/shard_map/reduce_sum | solution.py:177
  (108 shorter events, 34.5 us)
Async XLA Ops:
  6.5 88.6 %all-gather.6.cloned.1.call-start = ((), (), s32[]{:S(2)}) async-start(), calls=%async_computation.3 | async-start | bytes 4718592 | tf_op jit(solution)/shard_map/all_gather | solution.py:15
  16.2 18.9 %copy-start.9 = (f32[16]{0:T(128)S(1)}, f32[16]{0:T(128)}, u32[]{:S(2)}) copy-start(f32[16]{0:T(128)} %param.26) | copy-start | bytes 196
  23.2 0.8 copy-start.4
  24.0 160.7 %all-gather.8.cloned.1.call-start = ((), (), s32[]{:S(2)}) async-start(), calls=%async_computation.4 | async-start | bytes 6193152 | tf_op jit(solution)/shard_map/all_gather | solution.py:140
  24.7 175.8 %reduce-scatter.2.cloned.1.call-start = ((), (), s32[]{:S(2)}) async-start(), calls=%async_computation.5 | async-start | bytes 1032192 | tf_op jit(solution)/shard_map/reduce_scatter | solution.py:143
  95.1 36.7 %copy-start.3 = (bf16[128,1024]{1,0:T(8,128)(2,1)S(1)}, bf16[128,1024]{1,0:T(8,128)(2,1)}, u32[]{:S(2)}) copy-start(bf16[128,1024]{1,0:T(8,128)(2,1)} %param.20) | copy-start | bytes 786436
  95.1 36.7 %copy-start.5 = (bf16[128,1024]{1,0:T(8,128)(2,1)S(1)}, bf16[128,1024]{1,0:T(8,128)(2,1)}, u32[]{:S(2)}) copy-start(bf16[128,1024]{1,0:T(8,128)(2,1)} %param.21) | copy-start | bytes 786436
  131.2 53.4 %copy-start.10 = (f32[1024]{0:T(1024)S(1)}, f32[1024]{0:T(1024)}, u32[]{:S(2)}) copy-start(f32[1024]{0:T(1024)} %param.27) | copy-start | bytes 12292
  184.6 5.4 %copy-start.6 = (s32[64,6]{0,1:T(8,128)S(1)}, s32[64,6]{0,1:T(8,128)}, u32[]{:S(2)}) copy-start(s32[64,6]{0,1:T(8,128)} %param.32) | copy-start | bytes 4612
  184.6 15.9 %copy-start = (bf16[64,2688]{1,0:T(8,128)(2,1)S(1)}, bf16[64,2688]{1,0:T(8,128)(2,1)}, u32[]{:S(2)}) copy-start(bf16[64,2688]{1,0:T(8,128)(2,1)} %param.30) | copy-start | bytes 1032196
  184.6 17.1 %copy-start.7 = (f32[2688]{0:T(1024)S(1)}, f32[2688]{0:T(1024)}, u32[]{:S(2)}) copy-start(f32[2688]{0:T(1024)} %param.31) | copy-start | bytes 32260
  306.1 5.5 %copy-start.8 = (f32[64,6]{0,1:T(8,128)S(1)}, f32[64,6]{0,1:T(8,128)}, u32[]{:S(2)}) copy-start(f32[64,6]{0,1:T(8,128)} %param.33) | copy-start | bytes 4612
  306.1 81.6 %all-to-all-start.1 = ((bf16[16,36,2688]{2,1,0:T(8,128)(2,1)}), bf16[16,36,2688]{2,1,0:T(8,128)(2,1)}, u32[]{:S(2)}, u32[]{:S(2)}) async-start(bf16[16,36,2688]{2,1,0:T(8,128)(2,1)} %reshape.117), calls=%async_computation.2 | async-start | bytes 6881280 | tf_op jit(solution)/shard_map/all_to_all | solution.py:174
  398.6 4.6 %copy-start.1 = (bf16[64,2688]{1,0:T(8,128)(2,1)S(1)}, bf16[64,2688]{1,0:T(8,128)(2,1)}, u32[]{:S(2)}) copy-start(bf16[64,2688]{1,0:T(8,128)(2,1)} %param.30) | copy-start | bytes 1032196
  398.6 4.6 %copy-start.2 = (bf16[64,2688]{1,0:T(8,128)(2,1)S(1)}, bf16[64,2688]{1,0:T(8,128)(2,1)}, u32[]{:S(2)}) copy-start(bf16[64,2688]{1,0:T(8,128)(2,1)} %reduce-scatter.2.cloned.1.call-done) | copy-start | bytes 1032196
Sparse Core Ops, SparseCore 0:
  24.1 70.9 all-gather.5
  97.3 87.2 all-gather.7
  190.2 10.2 reduce-scatter.1
where the time goes:
time: 412 us; the launch traced here: 411 us
  waiting for transfers between devices  185 us (45%)
  blocking collectives  102 us (25%)
  local copies, waits for them, and re-layouts  34.4 us (8%)
  matrix products  24.1 us (6%)
  other arithmetic  23.5 us (6%)
  loops' own time  20.7 us (5%)
  between operations  15.1 us (4%)
  starting transfers between devices  5.37 us (1%)
    all_to_all x1, blocking collectives, local(): lax.all_to_all(outgoing, ('ctx', 'head'), split_axis=0, concat_axis=0, ti...  81.9 us
    all_to_all x1, waiting for transfers between devices, local(): lax.all_to_all(results, ('ctx', 'head'), split_axis=0, concat_axis=0, til...  76 us
    all_gather x1, waiting for transfers between devices, local(): lax.all_gather(w_out, 'ctx', axis=1, tiled=True)  51.6 us
    all_gather x1, waiting for transfers between devices, entering(): everything = jax.tree.map(lambda part: lax.all_gather(part, axis), array)  47.7 us
    another operation x1, loops' own time, entering(): return lax.fori_loop(0, size, lap, start)  20.6 us
    all_gather x1, blocking collectives, entering(): everything = jax.tree.map(lambda part: lax.all_gather(part, axis), array)  12.1 us
    reduce_scatter x1, waiting for transfers between devices, local(): lax.psum_scatter(partial_value.astype(jnp.bfloat16), 'head', scatter_dime...  9.49 us
    select_n x8, other arithmetic, lap(): return jax.tree.map(lambda a, b: jnp.where(reached, a, b), new, before)  9.42 us
  transfers between devices with their start and end apart: 4, of which 4 were waited for; matrix products, arithmetic and copies ran while one was open for 5% of the time, Pallas kernels for 0%

commit v1 on v0

--- a/solution.py
+++ b/solution.py
@@ -137,7 +137,7 @@
     normed_scan = (grouped.reshape(length, -1) * norm_gain).astype(jnp.bfloat16)
     partial_value = jnp.dot(
         normed_scan,
-        lax.all_gather(w_out, "ctx", axis=1, tiled=True),
+        jnp.concatenate(lax.all_gather(w_out, "ctx"), axis=1),
         preferred_element_type=jnp.float32,
     )
     mamba_out = lax.psum_scatter(

time: 412 us -> 422 us (1.024)
  local copies, waits for them, and re-layouts: 34.4 us -> 46 us
    unnamed x31 -> x32, local copies, waits for them, and re-layouts: 5.67 us -> 14.6 us
where the time goes in v1:
time: 422 us; the launch traced here: 420 us
  waiting for transfers between devices  187 us (44%)
  blocking collectives  102 us (24%)
  local copies, waits for them, and re-layouts  46 us (11%)
  other arithmetic  23.6 us (6%)
  matrix products  21.8 us (5%)
  loops' own time  19.6 us (5%)
  between operations  15.1 us (4%)
  starting transfers between devices  5.37 us (1%)
    all_to_all x1, blocking collectives, local(): lax.all_to_all(outgoing, ('ctx', 'head'), split_axis=0, concat_axis=0, ti...  81.9 us
    all_to_all x1, waiting for transfers between devices, local(): lax.all_to_all(results, ('ctx', 'head'), split_axis=0, concat_axis=0, til...  76 us
    all_gather x1, waiting for transfers between devices, local(): lax.all_gather(w_out, 'ctx')  53 us
    all_gather x1, waiting for transfers between devices, entering(): everything = jax.tree.map(lambda part: lax.all_gather(part, axis), array)  47.7 us
    another operation x1, loops' own time, entering(): return lax.fori_loop(0, size, lap, start)  19.5 us
    unnamed x32, local copies, waits for them, and re-layouts  14.6 us
    all_gather x1, blocking collectives, entering(): everything = jax.tree.map(lambda part: lax.all_gather(part, axis), array)  12.1 us
    reduce_scatter x1, waiting for transfers between devices, local(): lax.psum_scatter(partial_value.astype(jnp.bfloat16), 'head', scatter_dime...  9.49 us
  transfers between devices with their start and end apart: 4, of which 4 were waited for; matrix products, arithmetic and copies ran while one was open for 5% of the time, Pallas kernels for 0%

profile of v1, /device:TPU:13, one launch (start us, length us, event | category | flops | bytes accessed | tf_op | source)
XLA Modules:
  0.0 420.2 jit_solution(17152976964112434941)
XLA Ops:
  12.6 1.9 fusion.64
  16.2 6.9 %while.29 = (s32[]{:T(128)}, f32[2,128,8,64]{1,3,2,0:T(8,128)S(1)}, f32[2,8,64,128]{3,2,1,0:T(8,128)S(1)}, f32[2,128,8,64]{1,3,2,0:T(8,128)S(1)}, f32[2,128,8]{1...) while((s32[]{:T(128)}, f32[2,128,8,64]{1,3,2,0:T(8,128)S(1)}, ...), condition=%wide.region_2.3_spmd.clone, body=%wide.region_1.2_spmd.clone.sunk | while | flops 206162944 | bytes 1364705 | solution.py:109
  26.2 7.9 %all-reduce.2 = (s32[8]{0:T(128)S(1)}, s32[8]{0:T(128)S(1)}) all-reduce(s32[8]{0:T(128)S(1)} %get-tuple-element.359, s32[8]{0:T(128)S(1)} %slice_dynamic-update-slice_fusion), channel_id=2, replica_groups=mesh['parts'=2,'ctx'=8,'head'=2] {'ctx'}, use_global_device_ids=true, to_apply=%add | all-reduce | flops 16 | bytes 128
  35.3 12.1 %all-gather.3 = f32[8,1,16]{2,1,0:T(1,128)S(1)} all-gather(f32[1,1,16]{2,1,0:T(1,128)S(1)} %fusion.61), channel_id=1, replica_groups=mesh['parts'=2,'ctx'=8,'head'=2] {'ctx'}, dimensions={0}, use_global_device_ids=true | all-gather | bytes 576 | tf_op jit(solution)/shard_map/all_gather | solution.py:15
  47.4 47.7 %all-gather.7.cloned.1.call-done = f32[8,16,64,128]{3,2,1,0:T(8,128)} async-done(((f32[1,16,64,128]{3,2,1,0:T(8,128)}), f32[8,16,64,128]{3,2,1,0:T(8,128)}) %all-gather.7.cloned.1.call-update) | async-done | bytes 4194320 | tf_op jit(solution)/shard_map/all_gather | solution.py:15
  95.1 34.1 %while.30 = (s32[]{:T(128)}, s32[1]{0:T(128)}, f32[16,64,128]{2,1,0:T(8,128)S(1)}, s32[]{:T(128)}, s32[8,1]{0,1:T(1,128)S(1)}, /*index=5*/f32[8,16,64,128]{3,2,1...) while((s32[]{:T(128)}, s32[1]{0:T(128)}, ...), condition=%wide.region_4.5_spmd.clone, body=%wide.region_3.4_spmd.clone.sunk | while | flops 524317 | bytes 1573298 | solution.py:27
  131.6 53.0 %all-gather.9.cloned.1.call-done = bf16[8192,336]{0,1:T(8,128)(2,1)} async-done(((bf16[1024,336]{0,1:T(8,128)(2,1)}), bf16[8192,336]{0,1:T(8,128)(2,1)}) %all-gather.9.cloned.1.call-update) | async-done | bytes 5505040 | tf_op jit(solution)/shard_map/all_gather | solution.py:140
  184.6 8.9 %copy.117 = bf16[42,8,8,1024]{3,2,1,0:T(8,128)(2,1)S(1)} copy(bf16[42,8,8,1024]{3,1,2,0:T(8,128)(2,1)} %bitcast.145) | data formatting | bytes 11010048
  193.5 3.1 copy.106
  196.7 3.0 convolution_convert_fusion.1
  200.7 9.5 %reduce-scatter.2.cloned.1.call-done = bf16[64,2688]{1,0:T(8,128)(2,1)} async-done(((bf16[128,2688]{1,0:T(8,128)(2,1)}), bf16[64,2688]{1,0:T(8,128)(2,1)}) %reduce-scatter.2.cloned.1.call-update) | async-done | bytes 344080 | tf_op jit(solution)/shard_map/reduce_scatter | solution.py:143
  211.4 2.0 convolution_convert_fusion
  213.4 2.5 reshape.123
  215.9 81.9 %all_to_all.10 = bf16[16,36,2688]{2,1,0:T(8,128)(2,1)S(1)} all-to-all(bf16[16,36,2688]{2,1,0:T(8,128)(2,1)} %reshape.123), channel_id=1, replica_groups=mesh['parts'=2,'ctx'=8,'head'=2] {'ctx','head'}, dimensions={0} | all-to-all | bytes 6193152 | tf_op jit(solution)/shard_map/all_to_all | solution.py:170
  297.7 2.4 reshape.124
  300.1 6.9 %multiply_convert_fusion = bf16[576,928]{1,0:T(8,128)(2,1)S(1)} fusion(bf16[576,2688]{1,0:T(8,128)(2,1)} %reshape.124, bf16[1,2688,928]{1,2,0:T(8,128)(2,1)} %param.34), kind=kOutput, calls=%fused_computation.54 | convolution fusion | flops 2875226112 | bytes 9154560 | tf_op jit(solution)/shard_map/dot_general | solution.py:66
  307.0 6.2 %fusion.38 = bf16[576,2688]{1,0:T(8,128)(2,1)S(1)} fusion(bf16[576,928]{1,0:T(8,128)(2,1)S(1)} %multiply_convert_fusion, bf16[1,928,2688]{2,1,0:T(8,128)(2,1)} %param.35), kind=kOutput, calls=%fused_computation.51 | convolution fusion | flops 2875170816 | bytes 9154560 | tf_op jit(solution)/shard_map/dot_general | solution.py:68
  313.2 2.5 reshape.125
  315.7 5.3 %all-to-all-start.1 = ((bf16[16,36,2688]{2,1,0:T(8,128)(2,1)}), bf16[16,36,2688]{2,1,0:T(8,128)(2,1)}, u32[]{:S(2)}, u32[]{:S(2)}) async-start(bf16[16,36,2688]{2,1,0:T(8,128)(2,1)} %reshape.125), calls=%async_computation.2 | async-start | bytes 6881280 | tf_op jit(solution)/shard_map/all_to_all | solution.py:174
  321.4 76.0 %all-to-all-done.1 = bf16[16,36,2688]{2,1,0:T(8,128)(2,1)} async-done(((bf16[16,36,2688]{2,1,0:T(8,128)(2,1)}), bf16[16,36,2688]{2,1,0:T(8,128)(2,1)}, u32[]{:S(2)}, u32[]{:S(2)}) %all-to-all-start.1) | async-done | bytes 3096608 | tf_op jit(solution)/shard_map/all_to_all | solution.py:174
  397.3 3.0 reshape.126
  400.3 3.4 gather_fusion
  403.7 4.5 %reshape.142 = f32[64,6,2688]{2,1,0:T(8,128)} reshape(bf16[384,2688]{1,0:T(8,128)(2,1)} %gather_fusion) | data formatting | bytes 6193152 | tf_op jit(solution)/shard_map/convert_element_type | solution.py:176
  408.3 4.6 %multiply_reduce_fusion = f32[64,2688]{1,0:T(8,128)S(1)} fusion(f32[64,6,2688]{2,1,0:T(8,128)} %reshape.142, f32[64,6]{1,0:T(8,128)S(1)} %copy.110), kind=kLoop, calls=%fused_computation.46 | loop fusion | flops 1892352 | bytes 4818432 | tf_op jit(solution)/shard_map/reduce_sum | solution.py:177
  (110 shorter events, 37.3 us)
Async XLA Ops:
  6.5 88.6 %all-gather.7.cloned.1.call-start = ((), (), s32[]{:S(2)}) async-start(), calls=%async_computation.3 | async-start | bytes 4718592 | tf_op jit(solution)/shard_map/all_gather | solution.py:15
  16.2 18.9 %copy-start.9 = (f32[16]{0:T(128)S(1)}, f32[16]{0:T(128)}, u32[]{:S(2)}) copy-start(f32[16]{0:T(128)} %param.26) | copy-start | bytes 196
  23.2 0.8 copy-start.4
  24.0 160.6 %all-gather.9.cloned.1.call-start = ((), (), s32[]{:S(2)}) async-start(), calls=%async_computation.5 | async-start | bytes 6193152 | tf_op jit(solution)/shard_map/all_gather | solution.py:140
  24.7 185.4 %reduce-scatter.2.cloned.1.call-start = ((), (), s32[]{:S(2)}) async-start(), calls=%async_computation.4 | async-start | bytes 1032192 | tf_op jit(solution)/shard_map/reduce_scatter | solution.py:143
  95.1 35.2 %copy-start.3 = (bf16[128,1024]{1,0:T(8,128)(2,1)S(1)}, bf16[128,1024]{1,0:T(8,128)(2,1)}, u32[]{:S(2)}) copy-start(bf16[128,1024]{1,0:T(8,128)(2,1)} %param.20) | copy-start | bytes 786436
  95.1 35.3 %copy-start.5 = (bf16[128,1024]{1,0:T(8,128)(2,1)S(1)}, bf16[128,1024]{1,0:T(8,128)(2,1)}, u32[]{:S(2)}) copy-start(bf16[128,1024]{1,0:T(8,128)(2,1)} %param.21) | copy-start | bytes 786436
  193.5 3.1 copy-start.10
  196.6 3.1 copy-start.6
  196.6 13.5 %copy-start = (bf16[64,2688]{1,0:T(8,128)(2,1)S(1)}, bf16[64,2688]{1,0:T(8,128)(2,1)}, u32[]{:S(2)}) copy-start(bf16[64,2688]{1,0:T(8,128)(2,1)} %param.30) | copy-start | bytes 1032196
  196.7 14.7 %copy-start.7 = (f32[2688]{0:T(1024)S(1)}, f32[2688]{0:T(1024)}, u32[]{:S(2)}) copy-start(f32[2688]{0:T(1024)} %param.31) | copy-start | bytes 32260
  315.7 5.3 %copy-start.8 = (f32[64,6]{0,1:T(8,128)S(1)}, f32[64,6]{0,1:T(8,128)}, u32[]{:S(2)}) copy-start(f32[64,6]{0,1:T(8,128)} %param.33) | copy-start | bytes 4612
  315.7 81.6 %all-to-all-start.1 = ((bf16[16,36,2688]{2,1,0:T(8,128)(2,1)}), bf16[16,36,2688]{2,1,0:T(8,128)(2,1)}, u32[]{:S(2)}, u32[]{:S(2)}) async-start(bf16[16,36,2688]{2,1,0:T(8,128)(2,1)} %reshape.125), calls=%async_computation.2 | async-start | bytes 6881280 | tf_op jit(solution)/shard_map/all_to_all | solution.py:174
  408.3 4.6 %copy-start.1 = (bf16[64,2688]{1,0:T(8,128)(2,1)S(1)}, bf16[64,2688]{1,0:T(8,128)(2,1)}, u32[]{:S(2)}) copy-start(bf16[64,2688]{1,0:T(8,128)(2,1)} %param.30) | copy-start | bytes 1032196
  408.3 4.6 %copy-start.2 = (bf16[64,2688]{1,0:T(8,128)(2,1)S(1)}, bf16[64,2688]{1,0:T(8,128)(2,1)}, u32[]{:S(2)}) copy-start(bf16[64,2688]{1,0:T(8,128)(2,1)} %reduce-scatter.2.cloned.1.call-done) | copy-start | bytes 1032196
Sparse Core Ops, SparseCore 0:
  24.1 70.9 all-gather.6
  97.3 87.2 all-gather.8
  199.8 10.2 reduce-scatter.1
